TPU v7x, 256 devices: a whole 4x4x8 slice. The times are simulated.
256 devices in a mesh: seq: 32 (over y, z), grp: 8 (over x, core).
Axes of the slice: x: 4, y: 4, z: 8, core: 2. Of those that a mesh axis runs over, the one named last changes fastest.
Arguments:
- mixer_input: bfloat16 [5120, 32768], P('grp', 'seq'), may hold values from -5 to 5
- step_sizes: float32 [80, 32768], P('grp', 'seq'), may hold values from 0 to 1, as said below
- decay_rates: float32 [80], P('grp'), may hold values from 1 to 2
- skip_gain: float32 [80], P('grp'), may hold values from 0.5 to 1.5
- input_basis: bfloat16 [32768, 128], P('seq'), may hold values from -5 to 5
- output_basis: bfloat16 [32768, 128], P('seq'), may hold values from -0.5 to 0.5
- out_weight: bfloat16 [5120, 2560], P(None, 'grp'), may hold values from -0.078125 to 0.078125
Outputs:
- layer_output: bfloat16 [32768, 2560], P('seq', 'grp')
Inputs may be any that keep to these rules, and one draw needn't show every extreme that they name: `step_sizes`: positive step sizes.
All inputs are finite; a program needn't handle non-finite values.
Results may differ from a plain program's by a relative error of at most 0.0065.
Values may be sent and summed in bfloat16 or wider, within the bound.
A program may use at most 128 MiB of HBM per device.

v0:
```python
import jax
import jax.numpy as jnp
from jax import lax
from jax.sharding import PartitionSpec as P

HP = 64
N = 128
GROUP = 256


def entering_2(value, axis, combine, identity):
    peers, here = (lax.axis_size(axis), lax.axis_index(axis))
    everything = jax.tree.map(
        lambda part, kind: lax.all_gather(part.astype(kind), axis),
        value,
        (jnp.bfloat16, jnp.bfloat16),
    )
    start = jax.tree.map(
        lambda part, zero: jnp.broadcast_to(jnp.asarray(zero, part.dtype), part.shape),
        value,
        identity,
    )

    def lap(k, before):
        reached = k < here
        new = combine(
            before, jax.tree.map(lambda part, own: part[k].astype(own.dtype), everything, value)
        )
        return jax.tree.map(lambda a, b: jnp.where(reached, a, b), new, before)

    return lax.fori_loop(0, peers, lap, start)


def carry_in(total_log, final_state):
    total_decay = jnp.exp(total_log)

    def combine(earlier, later):
        return (earlier[0] * later[0], later[0][:, None, None] * earlier[1] + later[1])

    identity = (jnp.ones_like(total_decay), jnp.zeros_like(final_state))
    _, carried = entering_2((total_decay, final_state), "seq", combine, identity)
    return carried


def on_device(
    mixer_input, step_sizes, decay_rates, skip_gain, input_basis, output_basis, out_weight
):
    heads_here = step_sizes.shape[0]
    tokens_here = step_sizes.shape[1]
    count = tokens_here // GROUP
    channels = mixer_input.reshape(heads_here, HP, count, GROUP)
    log_decay = -(decay_rates[:, None] * step_sizes).reshape(heads_here, count, GROUP)
    steps_blocked = step_sizes.reshape(heads_here, count, GROUP)
    running = jnp.cumsum(log_decay, axis=2)
    basis_in_blocked = input_basis.reshape(count, GROUP, N)
    basis_out_blocked = output_basis.reshape(count, GROUP, N)
    gram = jnp.einsum(
        "cin,cjn->cij", basis_out_blocked, basis_in_blocked, preferred_element_type=jnp.float32
    )
    rows_index = lax.broadcasted_iota(jnp.int32, (GROUP, GROUP), 0)
    cols_index = lax.broadcasted_iota(jnp.int32, (GROUP, GROUP), 1)
    causal = rows_index >= cols_index
    gaps = running[:, :, :, None] - running[:, :, None, :]
    mixing = jnp.where(
        causal,
        gram[None] * jnp.exp(jnp.where(causal, gaps, 0.0)) * steps_blocked[:, :, None, :],
        0.0,
    ).astype(jnp.bfloat16)
    inner = jnp.einsum("hcij,hpcj->hpci", mixing, channels, preferred_element_type=jnp.float32)
    tail = jnp.exp(running[:, :, -1:] - running) * steps_blocked
    weighted_terms = (basis_in_blocked.astype(jnp.float32)[None] * tail[:, :, :, None]).astype(
        jnp.bfloat16
    )
    summaries = jnp.einsum(
        "hcjn,hpcj->chnp", weighted_terms, channels, preferred_element_type=jnp.float32
    )
    block_decay = jnp.exp(running[:, :, -1])

    def advance(state, pair):
        decay, digest_record = pair
        return (decay[:, None, None] * state + digest_record, state)

    zero_state = jnp.zeros((heads_here, N, HP), jnp.float32)
    final_state, entering = lax.scan(advance, zero_state, (block_decay.T, summaries))
    block_sums = jnp.sum(log_decay, axis=2)
    prefix = jnp.exp(jnp.cumsum(block_sums, axis=1) - block_sums)
    total_log = jnp.sum(block_sums, axis=1)
    basis_out_wide = basis_out_blocked.astype(jnp.float32)
    within = jnp.exp(running)[:, None]
    direct = skip_gain[:, None, None, None] * channels.astype(jnp.float32)
    carried = carry_in(total_log, final_state)
    states = entering + prefix.T[:, :, None, None] * carried[None]
    from_state = jnp.einsum(
        "cin,chnp->hpci", basis_out_wide, states, precision=lax.Precision.HIGHEST
    )
    mixed = inner + from_state * within + direct
    mixed_columns = mixed.astype(jnp.bfloat16).reshape(heads_here * HP, tokens_here)
    result = jnp.einsum(
        "kt,kd->td",
        lax.all_gather(mixed_columns, "grp", axis=0, tiled=True),
        out_weight,
        preferred_element_type=jnp.float32,
    )
    return result.astype(jnp.bfloat16)


def solution(mesh):
    placed = (
        P("grp", "seq"),
        P("grp", "seq"),
        P("grp"),
        P("grp"),
        P("seq", None),
        P("seq", None),
        P(None, "grp"),
    )
    return jax.shard_map(
        on_device, mesh=mesh, in_specs=placed, out_specs=P("seq", "grp"), check_vma=False
    )
```

profile of v0, /device:TPU:1, one launch (start us, length us, event | category | flops | bytes accessed | tf_op | source)
XLA Modules:
  0.0 377.4 jit_solution(3592990008132862632)
XLA Ops:
  14.0 5.1 %reduce-window.6 = f32[10,4,2,128]{3,0,1,2:T(8,128)} reduce-window(f32[10,4,2,128]{3,0,1,2:T(8,128)} %copy.30, f32[]{:T(128)} %constant.47.clone.1), window={size=1x1x1x128 pad=0_0x0_0x0_0x127_0}, to_apply=%region_0.0 | reduce-window | flops 1300480 | bytes 81924 | tf_op jit(solution)/shard_map/reduce-window
  27.5 3.8 %reshape.116 = bf16[10,64,4,256]{3,2,1,0:T(4,128)(2,1)} reshape(bf16[640,1024]{1,0:T(8,128)(2,1)} %param.11) | data formatting | bytes 2621440 | tf_op jit(solution)/shard_map/reshape | solution.py:51
  32.1 5.6 %fusion.9 = f32[4,10,128,64]{3,2,1,0:T(8,128)} fusion(f32[10,4,256]{2,0,1:T(8,128)} %copy.35, f32[4,256,128]{2,1,0:T(8,128)} %convert_element_type.64, bf16[10,64,4,256]{3,2,1,0:T(4,128)(2,1)} %reshape.116), kind=kOutput, calls=%fused_computation.17 | convolution fusion | flops 170393600 | bytes 3186688 | tf_op jit(solution)/shard_map/hcjn,hpcj->chnp/dot_general | solution.py:74
  37.8 15.7 %while.27 = (s32[]{:T(128)}, f32[10,128,64]{2,1,0:T(8,128)}, f32[4,10,128,64]{3,2,1,0:T(8,128)}, f32[4,10]{1,0:T(4,128)S(1)}, f32[4,10,128,64]{3,2,1,0:T(8,128)}, /*index=5*/s32[]{:T(128)}, s32[]{:T(128)}) while((s32[]{:T(128)}, f32[10,128,64]{2,1,0:T(8,128)}, f32[4,10,128,64]{3,2,1,0:T(8,128)}, f32[4,10]{1,0:T(4,128)S(1)}, ...), condition=%wide.region_3.4_spmd.clone, body=%wide.region_2.3_spmd.clone.sunk | while | flops 327683 | bytes 2294488 | solution.py:84
  42.7 2.3 bitcast_add_fusion.2
  47.0 2.3 bitcast_add_fusion.2
  51.2 2.3 bitcast_add_fusion.2
  58.5 64.9 %all-reduce = bf16[320]{0:T(512)(128)(2,1)S(1)} all-reduce(bf16[320]{0:T(512)(128)(2,1)S(1)} %dynamic-update-slice), channel_id=2, replica_groups=mesh['seq'=32,'grp'=8] {'seq'}, use_global_device_ids=true, to_apply=%add | all-reduce | flops 320 | bytes 1280
  127.2 2.2 fusion.23
  129.4 12.8 %all-gather.7.cloned.1.call-done = bf16[320,128,64]{1,2,0:T(8,128)(2,1)} async-done(((bf16[10,128,64]{1,2,0:T(8,128)(2,1)}), bf16[320,128,64]{1,2,0:T(8,128)(2,1)}) %all-gather.7.cloned.1.call-update) | async-done | bytes 5242896 | tf_op jit(solution)/shard_map/all_gather | solution.py:14
  142.2 149.2 %while.28 = (s32[]{:T(128)}, f32[10,128,64]{2,1,0:T(8,128)}, s32[]{:T(128)}, bf16[32,10]{1,0:T(8,128)(2,1)}, bf16[32,10,128,64]{2,3,1,0:T(8,128)(2,1)}, /*index=5*/s32[]{:T(128)}, s32[]{:T(128)}) while((s32[]{:T(128)}, f32[10,128,64]{2,1,0:T(8,128)}, s32[]{:T(128)}, bf16[32,10]{1,0:T(8,128)(2,1)}, ...), condition=%wide.region_8.9_spmd.clone, body=%wide.region_7.8_spmd.clone.sunk | while | flops 409614 | bytes 1474765 | solution.py:31
  149.2 2.2 fusion.33
  153.8 2.2 fusion.33
  158.5 2.2 fusion.33
  163.1 2.2 fusion.33
  219.3 2.2 fusion.33
  233.2 2.2 fusion.33
  247.1 2.2 fusion.33
  261.1 2.2 fusion.33
  279.8 2.2 fusion.33
  291.4 4.4 %fusion.13 = f32[4,10,64,256]{3,2,0,1:T(8,128)S(1)} fusion(bf16[4,256,128,1]{2,1,0,3:T(8,128)(2,1)} %bitcast.58, f32[4,10,128,64]{3,2,1,0:T(8,128)} %get-tuple-element.127, f32[10,128,64]{2,1,0:T(8,128)} %get-tuple-element.129, f32[4,10]{1,0:T(4,128)S(1)} %copy.38), kind=kOutput, calls=%fused_computation.22 | convolution fusion | flops 1007288320 | bytes 4522144 | tf_op jit(solution)/shard_map/cin,chnp->hpci/dot_general | solution.py:93
  295.9 4.0 %fusion.12 = bf16[10,64,4,256]{3,1,2,0:T(8,128)(2,1)S(1)} fusion(f32[4,10,64,256]{3,2,0,1:T(8,128)S(1)} %fusion.13, f32[10,4,256]{2,1,0:T(4,128)S(1)} %copy-done.6, f32[10,4,256]{2,1,0:T(4,128)S(1)} %copy-done.5, f32[4,256,256]{2,1,0:T(8,128)S(1)} %copy-done.2, pred[256,256]{1,0:T(8,128)(4,1)S(1)} %copy-done.7, bf16[10,64,4,256]{3,2,1,0:T(4,128)(2,1)S(1)} %copy-done.1, ...), kind=kOutput, calls=%fused_computation.21 | convolution fusion | flops 355205120 | bytes 6479912 | tf_op jit(solution)/shard_map/hcij,hpcj->hpci/dot_general | solution.py:69
  302.3 61.1 %all-gather.5.cloned.1.call-done = bf16[5120,1024]{1,0:T(8,128)(2,1)} async-done(((bf16[640,1024]{1,0:T(8,128)(2,1)}), bf16[5120,1024]{1,0:T(8,128)(2,1)}) %all-gather.5.cloned.1.call-update) | async-done | bytes 10485776 | tf_op jit(solution)/shard_map/all_gather | solution.py:100
  363.4 7.2 %convolution_convert_fusion = bf16[1024,320]{0,1:T(8,128)(2,1)} fusion(bf16[5120,320]{0,1:T(8,128)(2,1)S(1)} %copy-done, bf16[5120,1024]{1,0:T(8,128)(2,1)} %all-gather.5.cloned.1.call-done), kind=kOutput, calls=%fused_computation.27 | convolution fusion | flops 3355770880 | bytes 14417920 | tf_op jit(solution)/shard_map/kt,kd->td/dot_general | solution.py:98
  (192 shorter events, 165.7 us)
Async XLA Ops:
  6.5 356.9 %copy-start = (bf16[5120,320]{0,1:T(8,128)(2,1)S(1)}, bf16[5120,320]{0,1:T(8,128)(2,1)}, u32[]{:S(2)}) copy-start(bf16[5120,320]{0,1:T(8,128)(2,1)} %param.17) | copy-start | bytes 9830404
  6.5 24.7 %copy-start.3 = (bf16[1024,128]{1,0:T(8,128)(2,1)S(1)}, bf16[1024,128]{1,0:T(8,128)(2,1)}, u32[]{:S(2)}) copy-start(bf16[1024,128]{1,0:T(8,128)(2,1)} %param.15) | copy-start | bytes 786436
  6.5 135.6 %all-gather.7.cloned.1.call-start = ((), (), s32[]{:S(2)}) async-start(), calls=%async_computation.1 | async-start | bytes 5406720 | tf_op jit(solution)/shard_map/all_gather | solution.py:14
  9.8 0.6 copy-start.4
  37.8 19.2 %copy-start.11 = (u32[256]{0:T(256)S(1)}, u32[256]{0:T(256)}, u32[]{:S(2)}) copy-start(u32[256]{0:T(256)} %constant.56) | copy-start | bytes 3076
  37.8 20.5 %copy-start.9 = (f32[10]{0:T(128)S(1)}, f32[10]{0:T(128)}, u32[]{:S(2)}) copy-start(f32[10]{0:T(128)} %get-tuple-element.206) | copy-start | bytes 124
  55.4 308.0 %all-gather.5.cloned.1.call-start = ((), (), s32[]{:S(2)}) async-start(), calls=%async_computation | async-start | bytes 11796480 | tf_op jit(solution)/shard_map/all_gather | solution.py:100
  291.3 4.5 %copy-start.1 = (bf16[10,64,4,256]{3,2,1,0:T(4,128)(2,1)S(1)}, bf16[10,64,4,256]{3,2,1,0:T(4,128)(2,1)}, u32[]{:S(2)}) copy-start(bf16[10,64,4,256]{3,2,1,0:T(4,128)(2,1)} %reshape.116) | copy-start | bytes 3932164
  291.4 4.5 %copy-start.2 = (f32[4,256,256]{2,1,0:T(8,128)S(1)}, f32[4,256,256]{2,1,0:T(8,128)}, u32[]{:S(2)}) copy-start(f32[4,256,256]{2,1,0:T(8,128)} %fusion.23) | copy-start | bytes 3145732
  291.4 4.5 %copy-start.5 = (f32[10,4,256]{2,1,0:T(4,128)S(1)}, f32[10,4,256]{2,1,0:T(4,128)}, u32[]{:S(2)}) copy-start(f32[10,4,256]{2,1,0:T(4,128)} %reduce_window_sum.42) | copy-start | bytes 122884
  291.4 4.5 %copy-start.6 = (f32[10,4,256]{2,1,0:T(4,128)S(1)}, f32[10,4,256]{2,1,0:T(4,128)}, u32[]{:S(2)}) copy-start(f32[10,4,256]{2,1,0:T(4,128)} %mul.111) | copy-start | bytes 122884
  291.4 4.5 %copy-start.7 = (pred[256,256]{1,0:T(8,128)(4,1)S(1)}, pred[256,256]{1,0:T(8,128)(4,1)}, u32[]{:S(2)}) copy-start(pred[256,256]{1,0:T(8,128)(4,1)} %iota_compare_fusion) | copy-start | bytes 196612
  291.4 4.5 %copy-start.8 = (f32[10,4,256]{2,1,0:T(4,128)S(1)}, f32[10,4,256]{2,1,0:T(4,128)}, u32[]{:S(2)}) copy-start(f32[10,4,256]{2,1,0:T(4,128)} %get-tuple-element.208) | copy-start | bytes 122884
  291.4 4.5 %copy-start.10 = (f32[10]{0:T(128)S(1)}, f32[10]{0:T(128)}, u32[]{:S(2)}) copy-start(f32[10]{0:T(128)} %param.14) | copy-start | bytes 124
Sparse Core Ops, SparseCore 0:
  55.5 86.6 all-gather.6
  302.5 60.9 all-gather.4
where the time goes:
time: 381 us; the launch traced here: 377 us
  other arithmetic  120 us (31%)
  local copies, waits for them, and re-layouts  81.2 us (21%)
  waiting for transfers between devices  73.9 us (19%)
  blocking collectives  64.9 us (17%)
  matrix products  23.5 us (6%)
  between operations  14.2 us (4%)
    select_n x32, other arithmetic, lap(): return jax.tree.map(lambda a, b: jnp.where(reached, a, b), new, before)  68.9 us
    unnamed x1, blocking collectives  64.9 us
    all_gather x1, waiting for transfers between devices, on_device(): lax.all_gather(mixed_columns, 'grp', axis=0, tiled=True)  61.1 us
    dynamic_slice x64, local copies, waits for them, and re-layouts, lap(): part[k].astype(own.dtype)  58.7 us
    convert_element_type x32, other arithmetic, lap(): part[k].astype(own.dtype)  21.4 us
    all_gather x1, waiting for transfers between devices, entering_2(): lax.all_gather(part.astype(kind), axis)  12.8 us
    add x4, other arithmetic, advance(): return (decay[:, None, None] * state + digest_record, state)  8.81 us
  transfers between devices with their start and end apart: 2, of which 2 were waited for; matrix products, arithmetic and copies ran while one was open for 2% of the time, Pallas kernels for 0%

commit v1 on v0

--- a/solution.py
+++ b/solution.py
@@ -97,7 +97,9 @@
     mixed_columns = mixed.astype(jnp.bfloat16).reshape(heads_here * HP, tokens_here)
     result = jnp.einsum(
         "kt,kd->td",
-        lax.all_gather(mixed_columns, "grp", axis=0, tiled=True),
+        jnp.concatenate(
+            lax.all_to_all(jnp.stack([mixed_columns] * lax.axis_size("grp")), "grp", 0, 0), axis=0
+        ),
         out_weight,
         preferred_element_type=jnp.float32,
     )

time: 381 us -> 432 us (1.13)
  blocking collectives: 64.9 us -> 190 us
  waiting for transfers between devices: 73.9 us -> 12.8 us
  other arithmetic: 120 us -> 114 us
  local copies, waits for them, and re-layouts: 81.2 us -> 76.5 us
    all_to_all x0 -> x1, blocking collectives: none -> 125 us  [on_device(): lax.all_to_all(jnp.stack([mixed_columns] * lax.axis_size('grp')), 'grp',...]
    all_gather x1 -> x0, waiting for transfers between devices: 61.1 us -> none  [on_device(): lax.all_gather(mixed_columns, 'grp', axis=0, tiled=True)]
  transfers between devices with their start and end apart: 2 -> 1, of which waited for: 2 -> 1; matrix products, arithmetic and copies ran while one was open for 2% -> 2% of each run, Pallas kernels for 0% -> 0%
where the time goes in v1:
time: 432 us; the launch traced here: 429 us
  blocking collectives  190 us (44%)
  other arithmetic  114 us (26%)
  local copies, waits for them, and re-layouts  76.5 us (18%)
  matrix products  20.8 us (5%)
  between operations  14.3 us (3%)
  waiting for transfers between devices  12.8 us (3%)
    all_to_all x1, blocking collectives, on_device(): lax.all_to_all(jnp.stack([mixed_columns] * lax.axis_size('grp')), 'grp',...  125 us
    select_n x32, other arithmetic, lap(): return jax.tree.map(lambda a, b: jnp.where(reached, a, b), new, before)  68.9 us
    unnamed x1, blocking collectives  64.9 us
    dynamic_slice x64, local copies, waits for them, and re-layouts, lap(): part[k].astype(own.dtype)  58.7 us
    convert_element_type x32, other arithmetic, lap(): part[k].astype(own.dtype)  20.8 us
    all_gather x1, waiting for transfers between devices, entering_2(): lax.all_gather(part.astype(kind), axis)  12.8 us
    add x4, other arithmetic, advance(): return (decay[:, None, None] * state + digest_record, state)  8.81 us
  transfers between devices with their start and end apart: 1, of which 1 were waited for; matrix products, arithmetic and copies ran while one was open for 2% of the time, Pallas kernels for 0%

profile of v1, /device:TPU:1, one launch (start us, length us, event | category | flops | bytes accessed | tf_op | source)
XLA Modules:
  0.0 428.8 jit_solution(13872664467536664628)
XLA Ops:
  9.3 2.3 reduce-window.6
  14.7 3.8 reshape.118
  18.5 5.6 %fusion.9 = f32[4,10,128,64]{3,2,1,0:T(8,128)} fusion(f32[10,4,256]{2,0,1:T(8,128)S(1)} %copy.35, f32[4,256,128]{2,1,0:T(8,128)} %convert_element_type.64, bf16[10,64,4,256]{3,2,1,0:T(4,128)(2,1)} %reshape.118), kind=kOutput, calls=%fused_computation.17 | convolution fusion | flops 170393600 | bytes 3186688 | tf_op jit(solution)/shard_map/hcjn,hpcj->chnp/dot_general | solution.py:74
  24.1 15.7 %while.27 = (s32[]{:T(128)}, f32[10,128,64]{2,1,0:T(8,128)}, f32[4,10,128,64]{3,2,1,0:T(8,128)}, f32[4,10]{1,0:T(4,128)S(1)}, f32[4,10,128,64]{3,2,1,0:T(8,128)}, /*index=5*/s32[]{:T(128)}, s32[]{:T(128)}) while((s32[]{:T(128)}, f32[10,128,64]{2,1,0:T(8,128)}, f32[4,10,128,64]{3,2,1,0:T(8,128)}, f32[4,10]{1,0:T(4,128)S(1)}, ...), condition=%wide.region_3.4_spmd.clone, body=%wide.region_2.3_spmd.clone.sunk | while | flops 327683 | bytes 2293988 | solution.py:84
  29.1 2.3 bitcast_add_fusion.2
  33.4 2.3 bitcast_add_fusion.2
  37.6 2.3 bitcast_add_fusion.2
  44.9 64.9 %all-reduce = bf16[320]{0:T(512)(128)(2,1)S(1)} all-reduce(bf16[320]{0:T(512)(128)(2,1)S(1)} %dynamic-update-slice), channel_id=2, replica_groups=mesh['seq'=32,'grp'=8] {'seq'}, use_global_device_ids=true, to_apply=%add | all-reduce | flops 320 | bytes 1280
  113.6 2.2 fusion.23
  115.8 12.8 %all-gather.4.cloned.1.call-done = bf16[320,128,64]{1,2,0:T(8,128)(2,1)} async-done(((bf16[10,128,64]{1,2,0:T(8,128)(2,1)}), bf16[320,128,64]{1,2,0:T(8,128)(2,1)}) %all-gather.4.cloned.1.call-update) | async-done | bytes 5242896 | tf_op jit(solution)/shard_map/all_gather | solution.py:14
  128.6 148.6 %while.28 = (s32[]{:T(128)}, f32[10,128,64]{2,1,0:T(8,128)}, s32[]{:T(128)}, bf16[32,10]{1,0:T(8,128)(2,1)}, bf16[32,10,128,64]{2,3,1,0:T(8,128)(2,1)}, /*index=5*/s32[]{:T(128)}, s32[]{:T(128)}) while((s32[]{:T(128)}, f32[10,128,64]{2,1,0:T(8,128)}, s32[]{:T(128)}, bf16[32,10]{1,0:T(8,128)(2,1)}, ...), condition=%wide.region_8.9_spmd.clone, body=%wide.region_7.8_spmd.clone.sunk | while | flops 409614 | bytes 1474773 | solution.py:31
  149.7 2.2 fusion.33
  154.3 2.2 fusion.33
  159.0 2.2 fusion.33
  163.7 2.2 fusion.33
  182.2 2.2 fusion.33
  186.8 2.2 fusion.33
  205.3 2.2 fusion.33
  224.0 2.2 fusion.33
  277.2 4.5 %fusion.13 = f32[4,10,64,256]{3,2,0,1:T(8,128)S(1)} fusion(bf16[4,256,128,1]{2,1,0,3:T(8,128)(2,1)} %bitcast.60, f32[4,10,128,64]{3,2,1,0:T(8,128)} %get-tuple-element.127, f32[10,128,64]{2,1,0:T(8,128)} %get-tuple-element.129, f32[4,10]{1,0:T(4,128)S(1)} %copy.38), kind=kOutput, calls=%fused_computation.22 | convolution fusion | flops 1007288320 | bytes 4522144 | tf_op jit(solution)/shard_map/cin,chnp->hpci/dot_general | solution.py:93
  281.7 4.0 fusion.12
  287.0 5.3 %stack.3 = bf16[8,640,1024]{2,1,0:T(8,128)(2,1)} broadcast(bf16[640,1024]{1,0:T(8,128)(2,1)S(1)} %bitcast.56), dimensions={1,2} | broadcast | bytes 11796480 | tf_op jit(solution)/shard_map/stack | solution.py:101
  292.3 125.1 %all_to_all.5 = bf16[8,640,1024]{2,1,0:T(8,128)(2,1)S(1)} all-to-all(bf16[8,640,1024]{2,1,0:T(8,128)(2,1)} %stack.3), channel_id=1, replica_groups=mesh['seq'=32,'grp'=8] {'grp'}, dimensions={0} | all-to-all | bytes 20971520 | tf_op jit(solution)/shard_map/all_to_all | solution.py:101
  417.4 4.5 %convolution_convert_fusion = bf16[1024,320]{0,1:T(8,128)(2,1)} fusion(bf16[5120,320]{0,1:T(8,128)(2,1)S(1)} %copy-done, bf16[5120,1024]{1,0:T(8,128)(2,1)S(1)} %bitcast.54), kind=kOutput, calls=%fused_computation.27 | convolution fusion | flops 3355770880 | bytes 14417920 | tf_op jit(solution)/shard_map/kt,kd->td/dot_general | solution.py:98
  (193 shorter events, 155.3 us)
Async XLA Ops:
  6.5 410.9 %copy-start = (bf16[5120,320]{0,1:T(8,128)(2,1)S(1)}, bf16[5120,320]{0,1:T(8,128)(2,1)}, u32[]{:S(2)}) copy-start(bf16[5120,320]{0,1:T(8,128)(2,1)} %param.17) | copy-start | bytes 9830404
  6.5 122.0 %all-gather.4.cloned.1.call-start = ((), (), s32[]{:S(2)}) async-start(), calls=%async_computation.1 | async-start | bytes 5406720 | tf_op jit(solution)/shard_map/all_gather | solution.py:14
  7.6 16.6 %copy-start.7 = (f32[10,4,256]{2,1,0:T(4,128)}, f32[10,4,256]{2,1,0:T(4,128)S(1)}, u32[]{:S(2)}) copy-start(f32[10,4,256]{2,1,0:T(4,128)S(1)} %mul.111) | copy-start | bytes 122884
  8.6 0.6 copy-start.4
  12.0 12.1 %copy-start.5 = (f32[10,4,256]{2,1,0:T(4,128)}, f32[10,4,256]{2,1,0:T(4,128)S(1)}, u32[]{:S(2)}) copy-start(f32[10,4,256]{2,1,0:T(4,128)S(1)} %reduce_window_sum.42) | copy-start | bytes 122884
  24.1 19.1 %copy-start.12 = (u32[256]{0:T(256)S(1)}, u32[256]{0:T(256)}, u32[]{:S(2)}) copy-start(u32[256]{0:T(256)} %constant.56) | copy-start | bytes 3076
  24.1 89.4 %copy-start.3 = (bf16[1024,128]{1,0:T(8,128)(2,1)S(1)}, bf16[1024,128]{1,0:T(8,128)(2,1)}, u32[]{:S(2)}) copy-start(bf16[1024,128]{1,0:T(8,128)(2,1)} %param.15) | copy-start | bytes 786436
  277.1 4.5 %copy-start.1 = (bf16[10,64,4,256]{3,2,1,0:T(4,128)(2,1)S(1)}, bf16[10,64,4,256]{3,2,1,0:T(4,128)(2,1)}, u32[]{:S(2)}) copy-start(bf16[10,64,4,256]{3,2,1,0:T(4,128)(2,1)} %reshape.118) | copy-start | bytes 3932164
  277.1 4.5 %copy-start.2 = (f32[4,256,256]{2,1,0:T(8,128)S(1)}, f32[4,256,256]{2,1,0:T(8,128)}, u32[]{:S(2)}) copy-start(f32[4,256,256]{2,1,0:T(8,128)} %fusion.23) | copy-start | bytes 3145732
  277.1 4.5 %copy-start.6 = (f32[10,4,256]{2,1,0:T(4,128)S(1)}, f32[10,4,256]{2,1,0:T(4,128)}, u32[]{:S(2)}) copy-start(f32[10,4,256]{2,1,0:T(4,128)} %copy-done.5) | copy-start | bytes 122884
  277.1 4.5 %copy-start.8 = (f32[10,4,256]{2,1,0:T(4,128)S(1)}, f32[10,4,256]{2,1,0:T(4,128)}, u32[]{:S(2)}) copy-start(f32[10,4,256]{2,1,0:T(4,128)} %copy-done.7) | copy-start | bytes 122884
  277.1 4.5 %copy-start.9 = (pred[256,256]{1,0:T(8,128)(4,1)S(1)}, pred[256,256]{1,0:T(8,128)(4,1)}, u32[]{:S(2)}) copy-start(pred[256,256]{1,0:T(8,128)(4,1)} %iota_compare_fusion) | copy-start | bytes 196612
  277.2 4.5 %copy-start.10 = (f32[10,4,256]{2,1,0:T(4,128)S(1)}, f32[10,4,256]{2,1,0:T(4,128)}, u32[]{:S(2)}) copy-start(f32[10,4,256]{2,1,0:T(4,128)} %get-tuple-element.208) | copy-start | bytes 122884
  277.2 4.5 %copy-start.11 = (f32[10]{0:T(128)S(1)}, f32[10]{0:T(128)}, u32[]{:S(2)}) copy-start(f32[10]{0:T(128)} %param.14) | copy-start | bytes 124
Sparse Core Ops, SparseCore 0:
  41.9 86.6 all-gather.3
